TPU v7x, 512 devices: a whole 4x8x8 slice. The times are simulated.
512 devices in a mesh: space: 64 (over x, y, core), snap: 8 (over z).
Axes of the slice: x: 4, y: 8, z: 8, core: 2. Of those that a mesh axis runs over, the one named last changes fastest.
Arguments:
- velocity: bfloat16 [128, 3, 256, 32, 128], P('snap', None, 'space'), may hold values from -8 to 8
- metric: float32 [3, 256, 32, 128], P(None, 'space'), may hold values from 0.5 to 2
- volume: float32 [256, 32, 128], P('space'), may hold values from 0.3 to 9
- coeffs: bfloat16 [128, 128], replicated, may hold values from -0.5 to 0.5
Outputs:
- gram: float32 [128, 128], P('snap')
- modes: bfloat16 [128, 3, 256, 32, 128], P('snap', None, 'space')
All inputs are finite; a program needn't handle non-finite values.
Results may differ from a plain program's by a relative error of at most 0.0004.
The roundings to bfloat16 on the way count: a program that leaves them out, or rounds other values in their place, can miss the bound.
Values may be sent and summed in bfloat16 or wider, within the bound.
A program may use at most 64 MiB of HBM per device.

v0:
```python
import jax
import jax.numpy as jnp
from jax import lax
from jax.sharding import PartitionSpec as P

EPS = 1e-06


def with_halo(shard, sides, width):
    for axis, dim in sides:
        peers, length = (lax.axis_size(axis), shard.shape[dim])
        up = [(i, (i + 1) % peers) for i in range(peers)]
        down = [(j, i) for i, j in up]
        last = lax.slice_in_dim(shard, length - width, length, axis=dim)
        leading = lax.slice_in_dim(shard, 0, width, axis=dim)
        before = lax.ppermute(last, axis, up)
        after = lax.ppermute(leading, axis, down)
        shard = jnp.concatenate([before, shard, after], axis=dim)
    return shard


def deriv(padded, dim):
    count = padded.shape[dim] - 4

    def cut(offset):
        return lax.slice_in_dim(padded, offset, offset + count, axis=dim)

    return (8.0 * (cut(3) - cut(1)) - (cut(4) - cut(0))) / 12.0


def curl(padded_x, metric):
    inner = padded_x[:, :, 2:-2]
    padded_y = jnp.pad(inner, ((0, 0), (0, 0), (0, 0), (2, 2), (0, 0)))
    padded_z = jnp.concatenate([inner[..., -2:], inner, inner[..., :2]], axis=4)
    along_x = deriv(padded_x, 2) * metric[0]
    along_y = deriv(padded_y, 3) * metric[1]
    along_z = deriv(padded_z, 4) * metric[2]
    omega_x = along_y[:, 2] - along_z[:, 1]
    omega_y = along_z[:, 0] - along_x[:, 2]
    omega_z = along_x[:, 1] - along_y[:, 0]
    return jnp.stack([omega_x, omega_y, omega_z], axis=1).astype(jnp.bfloat16)


def per_device(velocity, metric, volume, coeffs):
    snap_dev = velocity.shape[0]
    snaps = coeffs.shape[0]
    group = lax.axis_index("snap")
    scale = 1.0 / (
        3.0 * volume.shape[0] * lax.axis_size("space") * volume.shape[1] * volume.shape[2]
    )
    padded = with_halo(velocity, (("space", 2),), 2)
    vorticity = curl(padded.astype(jnp.float32), metric)
    coeff_f = coeffs.astype(jnp.float32)
    moved = lax.all_to_all(vorticity, "snap", split_axis=3, concat_axis=0, tiled=True)
    part_y = moved.shape[3]
    vol_part = lax.dynamic_slice_in_dim(volume, group * part_y, part_y, 1)
    weighted = (moved.astype(jnp.float32) * vol_part).astype(jnp.bfloat16).reshape(snaps, -1)
    flat = moved.reshape(snaps, -1)
    partial_value = lax.dot_general(
        weighted, flat, (((1,), (1,)), ((), ())), preferred_element_type=jnp.float32
    )
    raw = lax.dot_general(
        coeffs, flat, (((0,), (0,)), ((), ())), preferred_element_type=jnp.float32
    )
    whole = lax.psum(partial_value, ("space", "snap")) * scale
    energy = jnp.sum(coeff_f * jnp.dot(whole, coeff_f, precision=lax.Precision.HIGHEST), axis=0)
    rows = lax.dynamic_slice_in_dim(whole, group * snap_dev, snap_dev, 0)
    local_modes = (raw / jnp.sqrt(energy + EPS)[:, None]).astype(jnp.bfloat16).reshape(moved.shape)
    modes = lax.all_to_all(local_modes, "snap", split_axis=0, concat_axis=3, tiled=True)
    return (rows, modes)


def solution(mesh):
    placed = (
        P("snap", None, "space", None, None),
        P(None, "space", None, None),
        P("space", None, None),
        P(),
    )
    return jax.shard_map(
        per_device,
        mesh=mesh,
        in_specs=placed,
        out_specs=(P("snap", None), P("snap", None, "space", None, None)),
        check_vma=False,
    )
```

profile of v0, /device:TPU:1, one launch (start us, length us, event | category | flops | bytes accessed | tf_op | source)
XLA Modules:
  0.0 432.7 jit_solution(15252249167389126826)
XLA Ops:
  7.2 1.8 fusion.21
  9.0 4.6 %collective-permute-start = (bf16[16,3,2,32,128]{4,3,2,1,0:T(8,128)(2,1)S(1)}, bf16[16,3,2,32,128]{4,3,2,1,0:T(8,128)(2,1)S(1)}, u32[]{:S(2)}, u32[]{:S(2)}) collective-permute-start(bf16[16,3,2,32,128]{4,3,2,1,0:T(8,128)(2,1)S(1)} %get-tuple-element.17), channel_id=1, source_target_pairs={{0,8},{8,16},{16,24},{24,32},{32,40},{40,48},{48,56},{56,64},{64,7... | collective-permute-start | bytes 2359304 | tf_op jit(solution)/shard_map/ppermute | solution.py:16
  13.6 6.1 %collective-permute-start.1 = (bf16[16,3,2,32,128]{4,3,2,1,0:T(8,128)(2,1)S(1)}, bf16[16,3,2,32,128]{4,3,2,1,0:T(8,128)(2,1)S(1)}, u32[]{:S(2)}, u32[]{:S(2)}) collective-permute-start(bf16[16,3,2,32,128]{4,3,2,1,0:T(8,128)(2,1)S(1)} %get-tuple-element.18), channel_id=1, source_target_pairs={{8,0},{16,8},{24,16},{32,24},{40,32},{48,40},{56,48},{64,56},{72,6... | collective-permute-start | bytes 2359304 | tf_op jit(solution)/shard_map/ppermute | solution.py:17
  19.7 1.0 copy.25
  20.9 1.6 collective-permute-done
  22.5 0.5 copy.24
  23.0 4.2 collective-permute-done.1
  27.2 0.5 copy.26
  27.7 0.4 maximum_convert_fusion
  28.2 2.8 fusion.20
  30.9 4.0 fusion.13
  34.9 16.7 %fusion.10 = (f32[16,3,4,32,128]{4,0,2,1,3:T(8,128)S(1)}, f32[16,3,4,32,128]{4,0,2,1,3:T(8,128)}) fusion(f32[16,3,4,32,2]{4,0,2,1,3:T(8,128)} %get-tuple-element.9, f32[16,3,4,32,128]{4,0,2,1,3:T(8,128)} %get-tuple-element.11, f32[16,3,4,32,2]{4,0,2,1,3:T(8,128)S(1)} %get-tuple-element.8, f32[4,32,128]{2,0,1:T(4,128)S(1)} %copy.28, f32[4,32,128]{2,0,1:T(4,128)S(1)} %copy.27), kind=kLoop, calls=%fused_computation.19 | loop fusion | flops 11010048 | bytes 9666560 | tf_op jit(solution)/shard_map/mul | solution.py:37
  51.6 2.3 fusion.19
  53.9 1.3 pad_maximum_fusion.2
  55.2 9.7 %all-to-all-start = ((bf16[16,3,4,32,128]{4,0,2,1,3:T(8,128)(2,1)}), bf16[16,3,4,32,128]{4,0,2,1,3:T(8,128)(2,1)S(1)}, u32[]{:S(2)}, u32[]{:S(2)}) async-start(bf16[16,3,4,32,128]{4,0,2,1,3:T(8,128)(2,1)} %pad_maximum_fusion.2), calls=%async_computation | async-start | bytes 3145728 | tf_op jit(solution)/shard_map/all_to_all | solution.py:54
  64.9 0.2 all-reduce.3.cloned.1.call-start
  65.2 40.2 %all-to-all-done = bf16[16,3,4,32,128]{4,0,2,1,3:T(8,128)(2,1)S(1)} async-done(((bf16[16,3,4,32,128]{4,0,2,1,3:T(8,128)(2,1)}), bf16[16,3,4,32,128]{4,0,2,1,3:T(8,128)(2,1)S(1)}, u32[]{:S(2)}, u32[]{:S(2)}) %all-to-all-start) | async-done | bytes 1572896 | tf_op jit(solution)/shard_map/all_to_all | solution.py:54
  105.4 1.2 copy.38
  106.6 2.4 multiply_convert_fusion
  109.0 3.8 convert_element_type.30
  112.8 1.2 reshape.34
  114.0 2.6 fusion.22
  116.6 258.8 %all-reduce.3.cloned.1.call-done = f32[128,128]{1,0:T(8,128)} async-done(((f32[128,128]{1,0:T(8,128)}), f32[128,128]{1,0:T(8,128)}) %all-reduce.3.cloned.1.call-update) | async-done | bytes 65552 | tf_op jit(solution)/shard_map/psum | solution.py:65
  375.5 1.0 fusion.16
  376.5 0.6 fusion
  377.2 2.5 copy.31
  379.6 3.6 all-to-all-start.1
  383.2 0.6 constant_dynamic-slice_fusion
  383.8 39.5 %all-to-all-done.1 = bf16[128,3,4,4,128]{4,3,2,1,0:T(4,128)(2,1)S(1)} async-done(((bf16[128,3,4,4,128]{4,3,2,1,0:T(4,128)(2,1)}), bf16[128,3,4,4,128]{4,3,2,1,0:T(4,128)(2,1)S(1)}, u32[]{:S(2)}, u32[]{:S(2)}) %all-to-all-start.1) | async-done | bytes 1572896 | tf_op jit(solution)/shard_map/all_to_all | solution.py:69
  423.4 0.4 copy.32
  423.8 0.4 copy.33
  424.3 1.6 copy.34
  (20 shorter events, 0.2 us)
Async XLA Ops:
  7.2 58.0 %copy-start = (f32[4,32,128]{2,1,0:T(8,128)S(1)}, f32[4,32,128]{2,1,0:T(8,128)}, u32[]{:S(2)}) copy-start(f32[4,32,128]{2,1,0:T(8,128)} %param.6) | copy-start | bytes 196612
  7.2 12.5 %copy-start.2 = (bf16[16,3,4,32,128]{4,3,2,1,0:T(8,128)(2,1)S(1)}, bf16[16,3,4,32,128]{4,3,2,1,0:T(8,128)(2,1)}, u32[]{:S(2)}) copy-start(bf16[16,3,4,32,128]{4,3,2,1,0:T(8,128)(2,1)} %param.4) | copy-start | bytes 4718596
  7.2 13.5 %copy-start.4 = (f32[3,4,32,128]{3,2,1,0:T(8,128)S(1)}, f32[3,4,32,128]{3,2,1,0:T(8,128)}, u32[]{:S(2)}) copy-start(f32[3,4,32,128]{3,2,1,0:T(8,128)} %param.5) | copy-start | bytes 589828
  9.0 13.5 %collective-permute-start = (bf16[16,3,2,32,128]{4,3,2,1,0:T(8,128)(2,1)S(1)}, bf16[16,3,2,32,128]{4,3,2,1,0:T(8,128)(2,1)S(1)}, u32[]{:S(2)}, u32[]{:S(2)}) collective-permute-start(bf16[16,3,2,32,128]{4,3,2,1,0:T(8,128)(2,1)S(1)} %get-tuple-element.17), channel_id=1, source_target_pairs={{0,8},{8,16},{16,24},{24,32},{32,40},{40,48},{48,56},{56,64},{64,7... | collective-permute-start | bytes 2359304 | tf_op jit(solution)/shard_map/ppermute | solution.py:16
  13.6 13.6 %collective-permute-start.1 = (bf16[16,3,2,32,128]{4,3,2,1,0:T(8,128)(2,1)S(1)}, bf16[16,3,2,32,128]{4,3,2,1,0:T(8,128)(2,1)S(1)}, u32[]{:S(2)}, u32[]{:S(2)}) collective-permute-start(bf16[16,3,2,32,128]{4,3,2,1,0:T(8,128)(2,1)S(1)} %get-tuple-element.18), channel_id=1, source_target_pairs={{8,0},{16,8},{24,16},{32,24},{40,32},{48,40},{56,48},{64,56},{72,6... | collective-permute-start | bytes 2359304 | tf_op jit(solution)/shard_map/ppermute | solution.py:17
  34.9 16.7 %copy-start.1 = (f32[16,3,4,32,128]{4,0,2,1,3:T(8,128)S(1)}, f32[16,3,4,32,128]{4,0,2,1,3:T(8,128)}, u32[]{:S(2)}) copy-start(f32[16,3,4,32,128]{4,0,2,1,3:T(8,128)} %get-tuple-element.10) | copy-start | bytes 9437188
  55.2 50.2 %all-to-all-start = ((bf16[16,3,4,32,128]{4,0,2,1,3:T(8,128)(2,1)}), bf16[16,3,4,32,128]{4,0,2,1,3:T(8,128)(2,1)S(1)}, u32[]{:S(2)}, u32[]{:S(2)}) async-start(bf16[16,3,4,32,128]{4,0,2,1,3:T(8,128)(2,1)} %pad_maximum_fusion.2), calls=%async_computation | async-start | bytes 3145728 | tf_op jit(solution)/shard_map/all_to_all | solution.py:54
  64.9 310.5 %all-reduce.3.cloned.1.call-start = ((), (), s32[]{:S(2)}) async-start(), calls=%async_computation.2 | async-start | bytes 131072 | tf_op jit(solution)/shard_map/psum | solution.py:65
  112.8 262.7 %copy-start.5 = (bf16[128,128]{1,0:T(8,128)(2,1)S(1)}, bf16[128,128]{1,0:T(8,128)(2,1)}, u32[]{:S(2)}) copy-start(bf16[128,128]{1,0:T(8,128)(2,1)} %param.7) | copy-start | bytes 98308
  377.1 6.1 %copy-start.3 = (f32[128,128]{1,0:T(8,128)S(1)}, f32[128,128]{1,0:T(8,128)}, u32[]{:S(2)}) copy-start(f32[128,128]{1,0:T(8,128)} %all-reduce.3.cloned.1.call-done) | copy-start | bytes 196612
  379.6 43.8 %all-to-all-start.1 = ((bf16[128,3,4,4,128]{4,3,2,1,0:T(4,128)(2,1)}), bf16[128,3,4,4,128]{4,3,2,1,0:T(4,128)(2,1)S(1)}, u32[]{:S(2)}, u32[]{:S(2)}) async-start(bf16[128,3,4,4,128]{4,3,2,1,0:T(4,128)(2,1)} %copy.31), calls=%async_computation.1 | async-start | bytes 3145728 | tf_op jit(solution)/shard_map/all_to_all | solution.py:69
Sparse Core Ops, SparseCore 0:
  116.8 258.6 all-reduce.2
where the time goes:
time: 433 us
  waiting for transfers between devices  344 us (79%)
  other arithmetic  27.1 us (6%)
  starting transfers between devices  24.2 us (6%)
  local copies, waits for them, and re-layouts  18.6 us (4%)
  between operations  14.2 us (3%)
    psum x1, waiting for transfers between devices, per_device(): whole = lax.psum(partial_value, ('space', 'snap')) * scale  259 us
    all_to_all x1, waiting for transfers between devices, per_device(): lax.all_to_all(vorticity, 'snap', split_axis=3, concat_axis=0, tiled=True)  40.2 us
    all_to_all x1, waiting for transfers between devices, per_device(): lax.all_to_all(local_modes, 'snap', split_axis=0, concat_axis=3, tiled=True)  39.5 us
    mul x2, other arithmetic, curl(): along_z = deriv(padded_z, 4) * metric[2]  16.7 us
    all_to_all x1, starting transfers between devices, per_device(): lax.all_to_all(vorticity, 'snap', split_axis=3, concat_axis=0, tiled=True)  9.74 us
  transfers between devices with their start and end apart: 5, of which 5 were waited for; matrix products, arithmetic and copies ran while one was open for 1% of the time, Pallas kernels for 0%

commit v1 on v0

v1 whole, which is shorter than its diff:
```python
import functools

import jax
import jax.numpy as jnp
from jax import lax
from jax.experimental import pallas as pl
from jax.experimental.pallas import tpu as pltpu
from jax.sharding import PartitionSpec as P

EPS = 1e-06
MESH = pl.DeviceIdType.MESH
F32 = jnp.float32
BF16 = jnp.bfloat16
HALF = 16
GROUP = 4


def remote(src, dst, send, recv, where):
    return pltpu.make_async_remote_copy(
        src_ref=src, dst_ref=dst, send_sem=send, recv_sem=recv,
        device_id=where, device_id_type=MESH,
    )


def kernel(
    ny, nz, nxc, cells,
    vel, metric, volume, coeffs,
    out, gram_out,
    ext, vort, got, raw, mbuf, coeff_t, acc, col, e_send, e_got, g_own, g_got0, g_send, g_got,
    local_sem, halo_ss, halo_rs, a_ss, a_rs, m_ss, m_rs, e_ss, e_rs, g_ss, g_rs,
):
    s = lax.axis_index("space")
    z = lax.axis_index("snap")
    nspace = ny * nxc
    core, iy, ix = lax.rem(s, 2), lax.rem(s // 2, ny), s // (2 * ny)
    q = ix * 2 + core
    left, right = lax.rem(s + nspace - 1, nspace), lax.rem(s + 1, nspace)

    def z_peer(k):
        return lax.rem(z + k, nz)

    def y_peer(k):
        return (ix * ny + lax.rem(iy + k, ny)) * 2 + core

    def q_peer(k):
        other = lax.rem(q + k, nxc)
        return ((other // 2) * ny + iy) * 2 + lax.rem(other, 2)

    barrier = pltpu.get_barrier_semaphore()
    for k in range(1, nz):
        pl.semaphore_signal(barrier, inc=1, device_id={"snap": z_peer(k)}, device_id_type=MESH)
    for k in range(1, ny):
        pl.semaphore_signal(barrier, inc=1, device_id={"space": y_peer(k)}, device_id_type=MESH)
    for k in range(1, nxc):
        pl.semaphore_signal(barrier, inc=1, device_id={"space": q_peer(k)}, device_id_type=MESH)
    for side in (left, right):
        pl.semaphore_signal(barrier, inc=1, device_id={"space": side}, device_id_type=MESH)

    loads = [
        pltpu.make_async_copy(vel.at[c], ext.at[c, 2:6, 2:34], local_sem.at[c]) for c in range(3)
    ]
    for c in (2, 1, 0):
        loads[c].start()
    blank = jnp.zeros((4, 2, 16, 128), BF16)
    for c in (0, 2):
        ext[c, 2:6, 0:2] = blank
        ext[c, 2:6, 34:36] = blank
    coeff_t[...] = coeffs[...].astype(F32).T.astype(BF16)
    acc[...] = jnp.zeros_like(acc)
    loads[2].wait()
    loads[1].wait()

    def tile(c, layer, row):
        return ext[c, layer, row].astype(F32)

    def stencil(a, b, c, d):
        return 8.0 * (c - b) - (d - a)

    def along_x(c, layer, row):
        return stencil(*[tile(c, layer + o, row + 2) for o in (0, 1, 3, 4)])

    def along_y(c, layer, row):
        return stencil(*[tile(c, layer + 2, row + o) for o in (0, 1, 3, 4)])

    def along_z(c, layer, row):
        f = tile(c, layer + 2, row + 2)
        return stencil(*[pltpu.roll(f, o % 128, 1) for o in (2, 1, -1, -2)])

    def factor(d, layer, row):
        return metric[d, layer, pl.ds(row, 1), :] * (1.0 / 12.0)

    def curl(c, layer, row):
        if c == 0:
            a = along_y(2, layer, row) * factor(1, layer, row)
            b = along_z(1, layer, row) * factor(2, layer, row)
        elif c == 1:
            a = along_z(0, layer, row) * factor(2, layer, row)
            b = along_x(2, layer, row) * factor(0, layer, row)
        else:
            a = along_x(1, layer, row) * factor(0, layer, row)
            b = along_y(0, layer, row) * factor(1, layer, row)
        return (a - b).astype(BF16)

    def place(part):
        return part // 2, lax.rem(part, 2) * HALF

    def part_curl(c, part):
        layer, low = place(part)

        def step(i, carry):
            for j in range(GROUP):
                row = low + i * GROUP + j
                vort[c, layer, row] = curl(c, layer, row)
            return carry

        lax.fori_loop(0, HALF // GROUP, step, 0)

    def part_send(c, k):
        peer = z_peer(k)
        layer, low = place(peer)
        return remote(
            vort.at[c, layer, pl.ds(low, HALF)], got.at[c, :, z],
            a_ss.at[c, k], a_rs.at[c, k], {"snap": peer},
        )

    def own_part(c):
        layer, low = place(z)
        return pltpu.make_async_copy(
            vort.at[c, layer, pl.ds(low, HALF)], got.at[c, :, z], a_ss.at[c, 0]
        )

    order = [k for pair in zip(range(nz // 2, 0, -1), range(nz // 2 + 1, nz + 1)) for k in pair]
    order = [k for k in order if k < nz]

    def exchange(c, after=None):
        if after is not None:
            for k in order:
                part_curl(c, z_peer(k))
            after()
            for k in order:
                part_send(c, k).start()
        else:
            for k in order:
                part_curl(c, z_peer(k))
                part_send(c, k).start()
        part_curl(c, z)
        own_part(c).start()

    def halo(c, side):
        n = 2 * (2 - c) + side
        if side == 0:
            return remote(
                ext.at[c, 2:4, 2:34], ext.at[c, 6:8, 2:34], halo_ss.at[n], halo_rs.at[n], {"space": left}
            )
        return remote(
            ext.at[c, 4:6, 2:34], ext.at[c, 0:2, 2:34], halo_ss.at[n], halo_rs.at[n], {"space": right}
        )

    def enter():
        pl.semaphore_wait(barrier, (nz - 1) + (ny - 1) + (nxc - 1) + 2)
        for c in (2, 1):
            for side in (0, 1):
                halo(c, side).start()

    exchange(0, enter)
    loads[0].wait()
    for c, needs in ((1, 2), (2, 1)):
        for side in (0, 1):
            halo(needs, side).wait_recv()
        exchange(c)

    my_layer, my_low = place(z)

    def wide(c, i):
        rows = [got[c, i * GROUP + j].reshape(128, 128) for j in range(GROUP)]
        return jnp.concatenate(rows, axis=1)

    def arrived(c):
        for k in order:
            part_send(c, k).wait_recv()
        own_part(c).wait()

    def gram_of(c):
        def step(i, carry):
            v = wide(c, i)
            cells_volume = jnp.concatenate(
                [volume[my_layer, pl.ds(my_low + i * GROUP + j, 1), :] for j in range(GROUP)], axis=1
            )
            w = (v.astype(F32) * cells_volume).astype(BF16)
            acc[...] += lax.dot_general(w, v, (((1,), (1,)), ((), ())), preferred_element_type=F32)
            return carry

        lax.fori_loop(0, HALF // GROUP, step, 0)

    def raw_of(c):
        def step(i, carry):
            r = jnp.dot(coeff_t[...], wide(c, i), preferred_element_type=F32)
            for j in range(GROUP):
                raw[c, i * GROUP + j] = r[:, 128 * j : 128 * (j + 1)]
            return carry

        lax.fori_loop(0, HALF // GROUP, step, 0)

    for c in range(3):
        arrived(c)
        gram_of(c)
        if c < 2:
            raw_of(c)

    g_own[...] = acc[...] * (1.0 / cells)
    coeff_f = coeffs[...].astype(F32)
    product = jnp.dot(g_own[...], coeff_f, precision=lax.Precision.HIGHEST, preferred_element_type=F32)
    partial_e = jnp.sum((product * coeff_f).reshape(16, 8, 128), axis=0)
    stages = (
        (nz, z, lambda k: {"snap": z_peer(k)}),
        (ny, iy, lambda k: {"space": y_peer(k)}),
        (nxc, q, lambda k: {"space": q_peer(k)}),
    )

    def e_copy(stage, k):
        _, mine, where = stages[stage]
        return remote(
            e_send.at[stage], e_got.at[stage, mine], e_ss.at[stage, k], e_rs.at[stage, k], where(k)
        )

    def g_copy0(k):
        peer = z_peer(k)
        return remote(
            g_own.at[pl.ds(pl.multiple_of(peer * 16, 16), 16)], g_got0.at[z],
            g_ss.at[0, k], g_rs.at[0, k], {"snap": peer},
        )

    def g_copy(stage, k):
        _, mine, where = stages[stage]
        return remote(
            g_send.at[stage], g_got.at[stage, mine], g_ss.at[stage, k], g_rs.at[stage, k], where(k)
        )

    for stage, (count, mine, _) in enumerate(stages):
        e_send[stage] = partial_e
        e_got[stage, mine] = partial_e
        for k in range(1, count):
            e_copy(stage, k).start()
        if stage == 0:
            for k in range(1, nz):
                g_copy0(k).start()
            raw_of(2)
        for k in range(1, count):
            e_copy(stage, k).wait_recv()
        partial_e = e_got[stage, 0]
        for i in range(1, count):
            partial_e = partial_e + e_got[stage, i]
    energy = jnp.sum(partial_e, axis=0, keepdims=True)
    inverse = 1.0 / jnp.sqrt(energy + EPS)
    at_row = lax.broadcasted_iota(jnp.int32, (128, 128), 0)
    at_lane = lax.broadcasted_iota(jnp.int32, (128, 128), 1)
    diagonal = jnp.where(at_row == at_lane, jnp.broadcast_to(inverse, (128, 128)), 0.0)
    col[...] = jnp.broadcast_to(jnp.sum(diagonal, axis=1, keepdims=True), (128, 128))

    def modes_for(group):
        first = pl.multiple_of(group * 16, 16)
        scale = col[pl.ds(first, 16), :]

        for c in range(3):
            def step(i, carry):
                for j in range(GROUP):
                    row = i * GROUP + j
                    mbuf[group, c, row] = (raw[c, row, pl.ds(first, 16), :] * scale).astype(BF16)
                return carry

            lax.fori_loop(0, HALF // GROUP, step, 0)

    def modes_copy(k):
        peer = z_peer(k)
        return remote(
            mbuf.at[peer], out.at[:, my_layer, pl.ds(my_low, HALF)],
            m_ss.at[k], m_rs.at[k], {"snap": peer},
        )

    for k in order:
        modes_for(z_peer(k))
        modes_copy(k).start()
    modes_for(z)
    own_modes = pltpu.make_async_copy(
        mbuf.at[z], out.at[:, my_layer, pl.ds(my_low, HALF)], m_ss.at[0]
    )
    own_modes.start()

    for k in range(1, nz):
        g_copy0(k).wait_recv()
    g_got0[z] = g_own[pl.ds(pl.multiple_of(z * 16, 16), 16), :]
    rows = g_got0[0]
    for i in range(1, nz):
        rows = rows + g_got0[i]
    for stage in (1, 2):
        count, mine, _ = stages[stage]
        g_send[stage] = rows
        g_got[stage, mine] = rows
        for k in range(1, count):
            g_copy(stage, k).start()
        for k in range(1, count):
            g_copy(stage, k).wait_recv()
        rows = g_got[stage, 0]
        for i in range(1, count):
            rows = rows + g_got[stage, i]
    gram_out[...] = rows

    own_modes.wait()
    for k in order:
        modes_copy(k).wait_recv()
    for c in (2, 1):
        for side in (0, 1):
            halo(c, side).wait_send()
    for k in order:
        for c in range(3):
            part_send(c, k).wait_send()
        modes_copy(k).wait_send()
        g_copy0(k).wait_send()
    for stage, (count, _, _) in enumerate(stages):
        for k in range(1, count):
            e_copy(stage, k).wait_send()
            if stage:
                g_copy(stage, k).wait_send()


def per_device(ny, nz, nxc, cells, velocity, metric, volume, coeffs):
    vel = jnp.transpose(velocity, (1, 2, 3, 0, 4))
    any_space = pl.BlockSpec(memory_space=pl.ANY)
    vmem = pl.BlockSpec(memory_space=pltpu.VMEM)
    top = max(nz, ny, nxc)
    dma = pltpu.SemaphoreType.DMA
    modes, rows = pl.pallas_call(
        functools.partial(kernel, ny, nz, nxc, cells),
        out_shape=(
            jax.ShapeDtypeStruct(vel.shape, BF16),
            jax.ShapeDtypeStruct((16, 128), F32),
        ),
        in_specs=[any_space, vmem, vmem, vmem],
        out_specs=(any_space, vmem),
        scratch_shapes=[
            pltpu.VMEM((3, 8, 36, 16, 128), BF16),
            pltpu.VMEM((3, 4, 32, 16, 128), BF16),
            pltpu.VMEM((3, HALF, nz, 16, 128), BF16),
            pltpu.VMEM((3, HALF, 128, 128), F32),
            pltpu.VMEM((nz, 3, HALF, 16, 128), BF16),
            pltpu.VMEM((128, 128), BF16),
            pltpu.VMEM((128, 128), F32),
            pltpu.VMEM((128, 128), F32),
            pltpu.VMEM((3, 8, 128), F32),
            pltpu.VMEM((3, top, 8, 128), F32),
            pltpu.VMEM((128, 128), F32),
            pltpu.VMEM((nz, 16, 128), F32),
            pltpu.VMEM((3, 16, 128), F32),
            pltpu.VMEM((3, top, 16, 128), F32),
            dma((3,)), dma((4,)), dma((4,)), dma((3, nz)), dma((3, nz)), dma((nz,)), dma((nz,)),
            dma((3, top)), dma((3, top)), dma((3, top)), dma((3, top)),
        ],
        compiler_params=pltpu.CompilerParams(
            collective_id=0, has_side_effects=True, vmem_limit_bytes=48 * 1024 * 1024
        ),
        name="pod",
    )(vel, metric, volume, coeffs)
    return rows, jnp.transpose(modes, (3, 0, 1, 2, 4))


def solution(mesh):
    nz = mesh.shape["snap"]
    nspace = mesh.shape["space"]
    ny = min(8, nspace // 2)
    placed = (
        P("snap", None, "space", None, None),
        P(None, "space", None, None),
        P("space", None, None),
        P(),
    )
    return jax.shard_map(
        functools.partial(per_device, ny, nz, nspace // ny, 3.0 * nspace * 4 * 32 * 128),
        mesh=mesh,
        in_specs=placed,
        out_specs=(P("snap", None), P("snap", None, "space", None, None)),
        check_vma=False,
    )
```

time: 433 us -> 108 us (0.25)
  waiting for transfers between devices: 344 us -> 0 us
  Pallas kernels: 0 us -> 103 us
  other arithmetic: 27.1 us -> 0 us
  starting transfers between devices: 24.2 us -> 0 us
  local copies, waits for them, and re-layouts: 18.6 us -> 4.63 us
  between operations: 14.2 us -> 0.69 us
    psum x1 -> x0, waiting for transfers between devices: 259 us -> none  [per_device(): whole = lax.psum(partial_value, ('space', 'snap')) * scale]
    pallas_call x0 -> x1, Pallas kernels: none -> 103 us  [per_device(): pl.pallas_call(functools.partial(kernel, ny, nz, nxc, cells), out_shape=(...]
    all_to_all x2 -> x0, waiting for transfers between devices: 79.7 us -> none  [the longest x1 40.2 us: per_device(): lax.all_to_all(vorticity, 'snap', split_axis=3, concat_axis=0, tiled=True)]
    mul x4 -> x0, other arithmetic: 20.7 us -> none  [the longest x2 16.7 us: curl(): along_z = deriv(padded_z, 4) * metric[2]]
    all_to_all x2 -> x0, starting transfers between devices: 13.3 us -> none  [the longest x1 9.74 us: per_device(): lax.all_to_all(vorticity, 'snap', split_axis=3, concat_axis=0, tiled=True)]
    ppermute x2 -> x0, starting transfers between devices: 10.7 us -> none  [the longest x1 6.08 us: with_halo(): after = lax.ppermute(leading, axis, down)]
    ppermute x2 -> x0, waiting for transfers between devices: 5.76 us -> none  [the longest x1 4.18 us: with_halo(): after = lax.ppermute(leading, axis, down)]
    slice x2 -> x0, local copies, waits for them, and re-layouts: 4.59 us -> none  [the longest x1 2.79 us: curl(): padded_z = jnp.concatenate([inner[..., -2:], inner, inner[..., :2]], axis=4)]
  transfers between devices with their start and end apart: 5 -> 0, of which waited for: 5 -> 0; matrix products, arithmetic and copies ran while one was open for 1% -> 0% of each run, Pallas kernels for 0% -> 0%
where the time goes in v1:
time: 108 us
  Pallas kernels  103 us (95%)
  local copies, waits for them, and re-layouts  4.63 us (4%)
    pallas_call x1, Pallas kernels, per_device(): pl.pallas_call(functools.partial(kernel, ny, nz, nxc, cells), out_shape=(...  103 us
    unnamed x9, local copies, waits for them, and re-layouts  4.63 us

profile of v1, /device:TPU:1, one launch (start us, length us, event | category | flops | bytes accessed | tf_op | source)
XLA Modules:
  0.0 108.2 jit_solution(2223577092378257862)
XLA Ops:
  0.6 0.0 copy-start.2
  0.6 0.0 copy-start.1
  0.7 0.0 copy-start
  0.7 2.5 %copy.9 = bf16[16,3,4,32,128]{4,0,3,2,1:T(8,128)(2,1)S(1)} copy(bf16[16,3,4,32,128]{4,3,2,1,0:T(8,128)(2,1)} %param.4) | data formatting | bytes 3145728 | tf_op args[0]
  3.1 0.0 copy-done.2
  3.1 0.0 copy-done.1
  3.1 0.0 copy-done
  3.2 102.9 %pod.1 = (bf16[3,4,32,16,128]{4,3,2,1,0:T(8,128)(2,1)S(1)}, f32[16,128]{1,0:T(8,128)S(1)}) custom-call(bf16[3,4,32,16,128]{4,3,2,1,0:T(8,128)(2,1)S(1)} %bitcast.4, f32[3,4,32,128]{3,2,1,0:T(8,128)S(1)} %copy-done, f32[4,32,128]{2,1,0:T(8,128)S(1)} %copy-done.1, bf16[128,128]{1,0:T(8,128)(2,1)S(1)} %copy-done.2), custom_call_target="tpu_custom_call" | custom-call | tf_op jit(solution)/shard_map/pod/pallas_call | solution.py:332
  106.1 1.6 %copy.7 = bf16[16,3,4,32,128]{4,3,2,1,0:T(8,128)(2,1)} copy(bf16[16,3,4,32,128]{4,0,3,2,1:T(8,128)(2,1)S(1)} %bitcast.5) | data formatting | bytes 3145728
  107.6 0.6 copy.11
Async XLA Ops:
  0.6 2.5 %copy-start.2 = (bf16[128,128]{1,0:T(8,128)(2,1)S(1)}, bf16[128,128]{1,0:T(8,128)(2,1)}, u32[]{:S(2)}) copy-start(bf16[128,128]{1,0:T(8,128)(2,1)} %coeffs.1) | copy-start | bytes 98308
  0.6 2.5 %copy-start.1 = (f32[4,32,128]{2,1,0:T(8,128)S(1)}, f32[4,32,128]{2,1,0:T(8,128)}, u32[]{:S(2)}) copy-start(f32[4,32,128]{2,1,0:T(8,128)} %volume.1) | copy-start | bytes 196612
  0.7 2.5 %copy-start = (f32[3,4,32,128]{3,2,1,0:T(8,128)S(1)}, f32[3,4,32,128]{3,2,1,0:T(8,128)}, u32[]{:S(2)}) copy-start(f32[3,4,32,128]{3,2,1,0:T(8,128)} %metric.1) | copy-start | bytes 589828

commit v2 on v1

--- a/solution.py
+++ b/solution.py
@@ -13,6 +13,7 @@
 BF16 = jnp.bfloat16
 HALF = 16
 GROUP = 4
+EARLY = 8
 
 
 def remote(src, dst, send, recv, where):
@@ -24,10 +25,11 @@
 
 def kernel(
     ny, nz, nxc, cells,
-    vel, metric, volume, coeffs,
+    vel, metric_in, volume_in, coeffs_in,
     out, gram_out,
-    ext, vort, got, raw, mbuf, coeff_t, acc, col, e_send, e_got, g_own, g_got0, g_send, g_got,
-    local_sem, halo_ss, halo_rs, a_ss, a_rs, m_ss, m_rs, e_ss, e_rs, g_ss, g_rs,
+    stage, metric, volume, coeffs, ext, vort, got, raw, mbuf, early, land, coeff_t, acc, col,
+    e_send, e_got, g_own, g_got0, g_send, g_got,
+    local_sem, halo_ss, halo_rs, a_ss, a_rs, m_ss, m_rs, f_ss, f_rs, e_ss, e_rs, g_ss, g_rs,
 ):
     s = lax.axis_index("space")
     z = lax.axis_index("snap")
@@ -56,19 +58,27 @@
     for side in (left, right):
         pl.semaphore_signal(barrier, inc=1, device_id={"space": side}, device_id_type=MESH)
 
-    loads = [
-        pltpu.make_async_copy(vel.at[c], ext.at[c, 2:6, 2:34], local_sem.at[c]) for c in range(3)
+    loads = [pltpu.make_async_copy(vel.at[:, c], stage.at[c], local_sem.at[c]) for c in range(3)]
+    tables = [
+        pltpu.make_async_copy(a, b, local_sem.at[3 + i])
+        for i, (a, b) in enumerate(((metric_in, metric), (coeffs_in, coeffs), (volume_in, volume)))
     ]
-    for c in (2, 1, 0):
-        loads[c].start()
+    for copy in (loads[2], loads[1], tables[0], loads[0], tables[1], tables[2]):
+        copy.start()
     blank = jnp.zeros((4, 2, 16, 128), BF16)
     for c in (0, 2):
         ext[c, 2:6, 0:2] = blank
         ext[c, 2:6, 34:36] = blank
-    coeff_t[...] = coeffs[...].astype(F32).T.astype(BF16)
     acc[...] = jnp.zeros_like(acc)
-    loads[2].wait()
-    loads[1].wait()
+
+    def load(c):
+        loads[c].wait()
+        for layer in range(4):
+            ext[c, 2 + layer, 2:34] = jnp.swapaxes(stage[c, :, layer], 0, 1)
+
+    load(2)
+    load(1)
+    tables[0].wait()
 
     def tile(c, layer, row):
         return ext[c, layer, row].astype(F32)
@@ -104,13 +114,17 @@
     def place(part):
         return part // 2, lax.rem(part, 2) * HALF
 
-    def part_curl(c, part):
+    def part_curl(c, part, own=False):
         layer, low = place(part)
 
         def step(i, carry):
             for j in range(GROUP):
-                row = low + i * GROUP + j
-                vort[c, layer, row] = curl(c, layer, row)
+                row = i * GROUP + j
+                value = curl(c, layer, low + row)
+                if own:
+                    got[c, row, z] = value
+                else:
+                    vort[c, layer, low + row] = value
             return carry
 
         lax.fori_loop(0, HALF // GROUP, step, 0)
@@ -123,28 +137,19 @@
             a_ss.at[c, k], a_rs.at[c, k], {"snap": peer},
         )
 
-    def own_part(c):
-        layer, low = place(z)
-        return pltpu.make_async_copy(
-            vort.at[c, layer, pl.ds(low, HALF)], got.at[c, :, z], a_ss.at[c, 0]
-        )
-
     order = [k for pair in zip(range(nz // 2, 0, -1), range(nz // 2 + 1, nz + 1)) for k in pair]
     order = [k for k in order if k < nz]
 
-    def exchange(c, after=None):
-        if after is not None:
-            for k in order:
-                part_curl(c, z_peer(k))
-            after()
-            for k in order:
+    def exchange(c, ahead=0, enter=None):
+        for n, k in enumerate(order):
+            part_curl(c, z_peer(k))
+            if enter is not None and n == ahead:
+                enter()
+                for earlier in order[:n]:
+                    part_send(c, earlier).start()
+            if enter is None or n >= ahead:
                 part_send(c, k).start()
-        else:
-            for k in order:
-                part_curl(c, z_peer(k))
-                part_send(c, k).start()
-        part_curl(c, z)
-        own_part(c).start()
+        part_curl(c, z, own=True)
 
     def halo(c, side):
         n = 2 * (2 - c) + side
@@ -162,8 +167,11 @@
             for side in (0, 1):
                 halo(c, side).start()
 
-    exchange(0, enter)
-    loads[0].wait()
+    exchange(0, 2, enter)
+    load(0)
+    for copy in tables[1:]:
+        copy.wait()
+    coeff_t[...] = coeffs[...].astype(F32).T.astype(BF16)
     for c, needs in ((1, 2), (2, 1)):
         for side in (0, 1):
             halo(needs, side).wait_recv()
@@ -178,7 +186,6 @@
     def arrived(c):
         for k in order:
             part_send(c, k).wait_recv()
-        own_part(c).wait()
 
     def gram_of(c):
         def step(i, carry):
@@ -236,20 +243,29 @@
             g_send.at[stage], g_got.at[stage, mine], g_ss.at[stage, k], g_rs.at[stage, k], where(k)
         )
 
-    for stage, (count, mine, _) in enumerate(stages):
-        e_send[stage] = partial_e
-        e_got[stage, mine] = partial_e
+    def early_copy(k):
+        peer = z_peer(k)
+        return remote(
+            raw.at[0, 0:EARLY, pl.ds(pl.multiple_of(peer * 16, 16), 16)], early.at[z],
+            f_ss.at[k], f_rs.at[k], {"snap": peer},
+        )
+
+    for step_of, (count, mine, _) in enumerate(stages):
+        e_send[step_of] = partial_e
+        e_got[step_of, mine] = partial_e
         for k in range(1, count):
-            e_copy(stage, k).start()
-        if stage == 0:
+            e_copy(step_of, k).start()
+        if step_of == 0:
+            for k in order:
+                early_copy(k).start()
             for k in range(1, nz):
                 g_copy0(k).start()
             raw_of(2)
         for k in range(1, count):
-            e_copy(stage, k).wait_recv()
-        partial_e = e_got[stage, 0]
+            e_copy(step_of, k).wait_recv()
+        partial_e = e_got[step_of, 0]
         for i in range(1, count):
-            partial_e = partial_e + e_got[stage, i]
+            partial_e = partial_e + e_got[step_of, i]
     energy = jnp.sum(partial_e, axis=0, keepdims=True)
     inverse = 1.0 / jnp.sqrt(energy + EPS)
     at_row = lax.broadcasted_iota(jnp.int32, (128, 128), 0)
@@ -257,34 +273,53 @@
     diagonal = jnp.where(at_row == at_lane, jnp.broadcast_to(inverse, (128, 128)), 0.0)
     col[...] = jnp.broadcast_to(jnp.sum(diagonal, axis=1, keepdims=True), (128, 128))
 
-    def modes_for(group):
+    def modes_for(group, own=False):
         first = pl.multiple_of(group * 16, 16)
         scale = col[pl.ds(first, 16), :]
 
-        for c in range(3):
-            def step(i, carry):
-                for j in range(GROUP):
-                    row = i * GROUP + j
-                    mbuf[group, c, row] = (raw[c, row, pl.ds(first, 16), :] * scale).astype(BF16)
-                return carry
-
-            lax.fori_loop(0, HALF // GROUP, step, 0)
-
-    def modes_copy(k):
+        def step(i, carry):
+            for c in range(3):
+                if c == 0 and not own:
+                    rows = [EARLY + i * (HALF - EARLY) // 4 + j for j in range((HALF - EARLY) // 4)]
+                else:
+                    rows = [i * GROUP + j for j in range(GROUP)]
+                for row in rows:
+                    value = (raw[c, row, pl.ds(first, 16), :] * scale).astype(BF16)
+                    if own:
+                        land[c, my_layer, my_low + row] = value
+                    else:
+                        mbuf[group, c, row] = value
+            return carry
+
+        lax.fori_loop(0, HALF // GROUP, step, 0)
+
+    def modes_copies(k):
         peer = z_peer(k)
-        return remote(
-            mbuf.at[peer], out.at[:, my_layer, pl.ds(my_low, HALF)],
-            m_ss.at[k], m_rs.at[k], {"snap": peer},
+        return (
+            remote(
+                mbuf.at[peer, 0, EARLY:HALF],
+                land.at[0, my_layer, pl.ds(my_low + EARLY, HALF - EARLY)],
+                m_ss.at[0, k], m_rs.at[0, k], {"snap": peer},
+            ),
+            remote(
+                mbuf.at[peer, 1:3], land.at[1:3, my_layer, pl.ds(my_low, HALF)],
+                m_ss.at[1, k], m_rs.at[1, k], {"snap": peer},
+            ),
         )
 
     for k in order:
         modes_for(z_peer(k))
-        modes_copy(k).start()
-    modes_for(z)
-    own_modes = pltpu.make_async_copy(
-        mbuf.at[z], out.at[:, my_layer, pl.ds(my_low, HALF)], m_ss.at[0]
-    )
-    own_modes.start()
+        for copy in modes_copies(k):
+            copy.start()
+    modes_for(z, own=True)
+
+    my_scale = col[pl.ds(pl.multiple_of(z * 16, 16), 16), :]
+    for k in order:
+        early_copy(k).wait_recv()
+        source = lax.rem(z + nz - k, nz)
+        layer, low = place(source)
+        for row in range(EARLY):
+            land[0, layer, low + row] = (early[source, row] * my_scale).astype(BF16)
 
     for k in range(1, nz):
         g_copy0(k).wait_recv()
@@ -292,39 +327,59 @@
     rows = g_got0[0]
     for i in range(1, nz):
         rows = rows + g_got0[i]
-    for stage in (1, 2):
-        count, mine, _ = stages[stage]
-        g_send[stage] = rows
-        g_got[stage, mine] = rows
+    for step_of in (1, 2):
+        count, mine, _ = stages[step_of]
+        g_send[step_of] = rows
+        g_got[step_of, mine] = rows
         for k in range(1, count):
-            g_copy(stage, k).start()
+            g_copy(step_of, k).start()
         for k in range(1, count):
-            g_copy(stage, k).wait_recv()
-        rows = g_got[stage, 0]
+            g_copy(step_of, k).wait_recv()
+        rows = g_got[step_of, 0]
         for i in range(1, count):
-            rows = rows + g_got[stage, i]
+            rows = rows + g_got[step_of, i]
     gram_out[...] = rows
 
-    own_modes.wait()
-    for k in order:
-        modes_copy(k).wait_recv()
+    def deliver(source):
+        layer, low = place(source)
+        rows_at = pl.ds(pl.multiple_of(low, HALF), HALF)
+        for c in range(3):
+            out[:, c, layer, rows_at, :] = jnp.swapaxes(land[c, layer, rows_at], 0, 1)
+
+    deliver(z)
+    for k in order[::-1]:
+        for copy in modes_copies(k):
+            copy.wait_recv()
+        deliver(lax.rem(z + nz - k, nz))
     for c in (2, 1):
         for side in (0, 1):
             halo(c, side).wait_send()
     for k in order:
         for c in range(3):
             part_send(c, k).wait_send()
-        modes_copy(k).wait_send()
+        for copy in modes_copies(k):
+            copy.wait_send()
+        early_copy(k).wait_send()
         g_copy0(k).wait_send()
-    for stage, (count, _, _) in enumerate(stages):
+    for step_of, (count, _, _) in enumerate(stages):
         for k in range(1, count):
-            e_copy(stage, k).wait_send()
-            if stage:
-                g_copy(stage, k).wait_send()
+            e_copy(step_of, k).wait_send()
+            if step_of:
+                g_copy(step_of, k).wait_send()
+
+
+def keep(modes, rows, modes_out, rows_out, sem):
+    copies = [
+        pltpu.make_async_copy(modes, modes_out, sem.at[0]),
+        pltpu.make_async_copy(rows, rows_out, sem.at[1]),
+    ]
+    for copy in copies:
+        copy.start()
+    for copy in copies:
+        copy.wait()
 
 
 def per_device(ny, nz, nxc, cells, velocity, metric, volume, coeffs):
-    vel = jnp.transpose(velocity, (1, 2, 3, 0, 4))
     any_space = pl.BlockSpec(memory_space=pl.ANY)
     vmem = pl.BlockSpec(memory_space=pltpu.VMEM)
     top = max(nz, ny, nxc)
@@ -332,17 +387,23 @@
     modes, rows = pl.pallas_call(
         functools.partial(kernel, ny, nz, nxc, cells),
         out_shape=(
-            jax.ShapeDtypeStruct(vel.shape, BF16),
+            jax.ShapeDtypeStruct(velocity.shape, BF16),
             jax.ShapeDtypeStruct((16, 128), F32),
         ),
-        in_specs=[any_space, vmem, vmem, vmem],
-        out_specs=(any_space, vmem),
+        in_specs=[any_space] * 4,
+        out_specs=(vmem, vmem),
         scratch_shapes=[
+            pltpu.VMEM((3, 16, 4, 32, 128), BF16),
+            pltpu.VMEM(metric.shape, F32),
+            pltpu.VMEM(volume.shape, F32),
+            pltpu.VMEM(coeffs.shape, BF16),
             pltpu.VMEM((3, 8, 36, 16, 128), BF16),
             pltpu.VMEM((3, 4, 32, 16, 128), BF16),
             pltpu.VMEM((3, HALF, nz, 16, 128), BF16),
             pltpu.VMEM((3, HALF, 128, 128), F32),
             pltpu.VMEM((nz, 3, HALF, 16, 128), BF16),
+            pltpu.VMEM((nz, EARLY, 16, 128), F32),
+            pltpu.VMEM((3, 4, 32, 16, 128), BF16),
             pltpu.VMEM((128, 128), BF16),
             pltpu.VMEM((128, 128), F32),
             pltpu.VMEM((128, 128), F32),
@@ -352,15 +413,28 @@
             pltpu.VMEM((nz, 16, 128), F32),
             pltpu.VMEM((3, 16, 128), F32),
             pltpu.VMEM((3, top, 16, 128), F32),
-            dma((3,)), dma((4,)), dma((4,)), dma((3, nz)), dma((3, nz)), dma((nz,)), dma((nz,)),
+            dma((6,)), dma((4,)), dma((4,)), dma((3, nz)), dma((3, nz)), dma((2, nz)), dma((2, nz)),
+            dma((nz,)), dma((nz,)),
             dma((3, top)), dma((3, top)), dma((3, top)), dma((3, top)),
         ],
         compiler_params=pltpu.CompilerParams(
             collective_id=0, has_side_effects=True, vmem_limit_bytes=48 * 1024 * 1024
         ),
         name="pod",
-    )(vel, metric, volume, coeffs)
-    return rows, jnp.transpose(modes, (3, 0, 1, 2, 4))
+    )(*[pltpu.with_memory_space_constraint(a, pltpu.HBM) for a in (velocity, metric, volume, coeffs)])
+    modes, rows = pl.pallas_call(
+        keep,
+        out_shape=(
+            jax.ShapeDtypeStruct(modes.shape, BF16),
+            jax.ShapeDtypeStruct(rows.shape, F32),
+        ),
+        in_specs=[any_space, any_space],
+        out_specs=(any_space, any_space),
+        scratch_shapes=[dma((2,))],
+        compiler_params=pltpu.CompilerParams(vmem_limit_bytes=1024 * 1024),
+        name="keep",
+    )(modes, rows)
+    return rows, modes
 
 
 def solution(mesh):

time: 108 us -> 102 us (0.944)
  local copies, waits for them, and re-layouts: 4.63 us -> 0 us
  Pallas kernels: 103 us -> 101 us
    unnamed x9 -> x0, local copies, waits for them, and re-layouts: 4.63 us -> none
    pallas_call x1, Pallas kernels: 103 us -> 99.8 us  [per_device(): pl.pallas_call(functools.partial(kernel, ny, nz, nxc, cells), out_shape=(...]
    pallas_call x0 -> x1, Pallas kernels: none -> 1.16 us  [per_device(): pl.pallas_call(keep, out_shape=(jax.ShapeDtypeStruct(modes.shape, BF16),...]
where the time goes in v2:
time: 102 us
  Pallas kernels  101 us (99%)
    pallas_call x1, Pallas kernels, per_device(): pl.pallas_call(functools.partial(kernel, ny, nz, nxc, cells), out_shape=(...  99.8 us

profile of v2, /device:TPU:1, one launch (start us, length us, event | category | flops | bytes accessed | tf_op | source)
XLA Modules:
  0.0 101.6 jit_solution(16590854972194920593)
XLA Ops:
  0.6 99.8 %pod.1 = (bf16[16,3,4,32,128]{4,3,2,1,0:T(8,128)(2,1)S(1)}, f32[16,128]{1,0:T(8,128)S(1)}) custom-call(bf16[16,3,4,32,128]{4,3,2,1,0:T(8,128)(2,1)} %vel.1, f32[3,4,32,128]{3,2,1,0:T(8,128)} %metric_in.1, f32[4,32,128]{2,1,0:T(8,128)} %volume_in.1, bf16[128,128]{1,0:T(8,128)(2,1)} %coeffs_in.1), custom_call_target="tpu_custom_call" | custom-call | tf_op jit(solution)/shard_map/pod/pallas_call | solution.py:387
  100.5 1.2 %keep.1 = (bf16[16,3,4,32,128]{4,3,2,1,0:T(8,128)(2,1)}, f32[16,128]{1,0:T(8,128)}) custom-call(bf16[16,3,4,32,128]{4,3,2,1,0:T(8,128)(2,1)S(1)} %get-tuple-element.6.modes, f32[16,128]{1,0:T(8,128)S(1)} %get-tuple-element.7.rows), custom_call_target="tpu_custom_call" | custom-call | tf_op jit(solution)/shard_map/keep/pallas_call | solution.py:425

commit v3 on v2

--- a/solution.py
+++ b/solution.py
@@ -13,6 +13,7 @@
 BF16 = jnp.bfloat16
 HALF = 16
 GROUP = 4
+PIECES = ((0, 0, 16), (1, 0, 16), (2, 0, 12), (2, 12, 4))
 EARLY = 8
 
 
@@ -28,7 +29,7 @@
     vel, metric_in, volume_in, coeffs_in,
     out, gram_out,
     stage, metric, volume, coeffs, ext, vort, got, raw, mbuf, early, land, coeff_t, acc, col,
-    e_send, e_got, g_own, g_got0, g_send, g_got,
+    e_send, e_got, g_own, g_send, g_got,
     local_sem, halo_ss, halo_rs, a_ss, a_rs, m_ss, m_rs, f_ss, f_rs, e_ss, e_rs, g_ss, g_rs,
 ):
     s = lax.axis_index("space")
@@ -114,12 +115,13 @@
     def place(part):
         return part // 2, lax.rem(part, 2) * HALF
 
-    def part_curl(c, part, own=False):
+    def part_curl(piece, part, own=False):
+        c, first, count = piece
         layer, low = place(part)
 
         def step(i, carry):
             for j in range(GROUP):
-                row = i * GROUP + j
+                row = first + i * GROUP + j
                 value = curl(c, layer, low + row)
                 if own:
                     got[c, row, z] = value
@@ -127,29 +129,31 @@
                     vort[c, layer, low + row] = value
             return carry
 
-        lax.fori_loop(0, HALF // GROUP, step, 0)
-
-    def part_send(c, k):
+        lax.fori_loop(0, count // GROUP, step, 0)
+
+    def part_send(piece, k):
+        c, first, count = piece
+        n = PIECES.index(piece)
         peer = z_peer(k)
         layer, low = place(peer)
         return remote(
-            vort.at[c, layer, pl.ds(low, HALF)], got.at[c, :, z],
-            a_ss.at[c, k], a_rs.at[c, k], {"snap": peer},
+            vort.at[c, layer, pl.ds(low + first, count)], got.at[c, first : first + count, z],
+            a_ss.at[n, k], a_rs.at[n, k], {"snap": peer},
         )
 
     order = [k for pair in zip(range(nz // 2, 0, -1), range(nz // 2 + 1, nz + 1)) for k in pair]
     order = [k for k in order if k < nz]
 
-    def exchange(c, ahead=0, enter=None):
+    def exchange(piece, ahead=0, enter=None):
         for n, k in enumerate(order):
-            part_curl(c, z_peer(k))
+            part_curl(piece, z_peer(k))
             if enter is not None and n == ahead:
                 enter()
                 for earlier in order[:n]:
-                    part_send(c, earlier).start()
+                    part_send(piece, earlier).start()
             if enter is None or n >= ahead:
-                part_send(c, k).start()
-        part_curl(c, z, own=True)
+                part_send(piece, k).start()
+        part_curl(piece, z, own=True)
 
     def halo(c, side):
         n = 2 * (2 - c) + side
@@ -167,7 +171,7 @@
             for side in (0, 1):
                 halo(c, side).start()
 
-    exchange(0, 2, enter)
+    exchange(PIECES[0], 2, enter)
     load(0)
     for copy in tables[1:]:
         copy.wait()
@@ -175,7 +179,9 @@
     for c, needs in ((1, 2), (2, 1)):
         for side in (0, 1):
             halo(needs, side).wait_recv()
-        exchange(c)
+        for piece in PIECES:
+            if piece[0] == c:
+                exchange(piece)
 
     my_layer, my_low = place(z)
 
@@ -183,11 +189,13 @@
         rows = [got[c, i * GROUP + j].reshape(128, 128) for j in range(GROUP)]
         return jnp.concatenate(rows, axis=1)
 
-    def arrived(c):
+    def arrived(piece):
         for k in order:
-            part_send(c, k).wait_recv()
-
-    def gram_of(c):
+            part_send(piece, k).wait_recv()
+
+    def gram_of(piece):
+        c, first, count = piece
+
         def step(i, carry):
             v = wide(c, i)
             cells_volume = jnp.concatenate(
@@ -197,7 +205,7 @@
             acc[...] += lax.dot_general(w, v, (((1,), (1,)), ((), ())), preferred_element_type=F32)
             return carry
 
-        lax.fori_loop(0, HALF // GROUP, step, 0)
+        lax.fori_loop(first // GROUP, (first + count) // GROUP, step, 0)
 
     def raw_of(c):
         def step(i, carry):
@@ -208,11 +216,11 @@
 
         lax.fori_loop(0, HALF // GROUP, step, 0)
 
-    for c in range(3):
-        arrived(c)
-        gram_of(c)
-        if c < 2:
-            raw_of(c)
+    for piece in PIECES:
+        arrived(piece)
+        gram_of(piece)
+        if piece[0] < 2:
+            raw_of(piece[0])
 
     g_own[...] = acc[...] * (1.0 / cells)
     coeff_f = coeffs[...].astype(F32)
@@ -230,18 +238,32 @@
             e_send.at[stage], e_got.at[stage, mine], e_ss.at[stage, k], e_rs.at[stage, k], where(k)
         )
 
-    def g_copy0(k):
-        peer = z_peer(k)
+    def g_rows(k):
+        peer = lax.rem(iy + k, ny)
         return remote(
-            g_own.at[pl.ds(pl.multiple_of(peer * 16, 16), 16)], g_got0.at[z],
-            g_ss.at[0, k], g_rs.at[0, k], {"snap": peer},
-        )
-
-    def g_copy(stage, k):
-        _, mine, where = stages[stage]
+            g_own.at[pl.ds(pl.multiple_of(peer * 16, 16), 16)], g_got.at[0, iy],
+            g_ss.at[0, k], g_rs.at[0, k], {"space": y_peer(k)},
+        )
+
+    def g_across(k):
         return remote(
-            g_send.at[stage], g_got.at[stage, mine], g_ss.at[stage, k], g_rs.at[stage, k], where(k)
-        )
+            g_send.at[0], g_got.at[1, q], g_ss.at[1, k], g_rs.at[1, k], {"space": q_peer(k)}
+        )
+
+    def g_along(k):
+        return remote(g_send.at[1], g_got.at[2, z], g_ss.at[2, k], g_rs.at[2, k], {"snap": z_peer(k)})
+
+    def g_back(k):
+        return remote(g_send.at[2], gram_out, g_ss.at[3, k], g_rs.at[3, k], {"space": y_peer(k)})
+
+    def total(which, count):
+        rows = g_got[which, 0]
+        for i in range(1, count):
+            rows = rows + g_got[which, i]
+        return rows
+
+    home = z == iy
+    to_home = lax.rem(iy + nz - z, nz)
 
     def early_copy(k):
         peer = z_peer(k)
@@ -253,14 +275,34 @@
     for step_of, (count, mine, _) in enumerate(stages):
         e_send[step_of] = partial_e
         e_got[step_of, mine] = partial_e
-        for k in range(1, count):
+        for k in order:
             e_copy(step_of, k).start()
         if step_of == 0:
+            for k in range(1, ny):
+                g_rows(k).start()
+            raw_of(2)
+        if step_of == 1:
             for k in order:
                 early_copy(k).start()
-            for k in range(1, nz):
-                g_copy0(k).start()
-            raw_of(2)
+            g_got[0, iy] = g_own[pl.ds(pl.multiple_of(iy * 16, 16), 16), :]
+            for k in range(1, ny):
+                g_rows(k).wait_recv()
+            rows = total(0, ny)
+            g_send[0] = rows
+            g_got[1, q] = rows
+            for k in range(1, nxc):
+                g_across(k).start()
+        if step_of == 2:
+            for k in range(1, nxc):
+                g_across(k).wait_recv()
+            rows = total(1, nxc)
+            g_send[1] = rows
+            g_got[2, z] = rows
+
+            @pl.when(jnp.logical_not(home))
+            def _():
+                g_along(to_home).start()
+
         for k in range(1, count):
             e_copy(step_of, k).wait_recv()
         partial_e = e_got[step_of, 0]
@@ -277,20 +319,21 @@
         first = pl.multiple_of(group * 16, 16)
         scale = col[pl.ds(first, 16), :]
 
+        def put(c, row):
+            value = (raw[c, row, pl.ds(first, 16), :] * scale).astype(BF16)
+            if own:
+                land[c, my_layer, my_low + row] = value
+            else:
+                mbuf[group, c, row] = value
+
         def step(i, carry):
-            for c in range(3):
-                if c == 0 and not own:
-                    rows = [EARLY + i * (HALF - EARLY) // 4 + j for j in range((HALF - EARLY) // 4)]
-                else:
-                    rows = [i * GROUP + j for j in range(GROUP)]
-                for row in rows:
-                    value = (raw[c, row, pl.ds(first, 16), :] * scale).astype(BF16)
-                    if own:
-                        land[c, my_layer, my_low + row] = value
-                    else:
-                        mbuf[group, c, row] = value
+            for c in (1, 2):
+                for j in range(GROUP):
+                    put(c, i * GROUP + j)
             return carry
 
+        for row in range(0 if own else EARLY, HALF):
+            put(0, row)
         lax.fori_loop(0, HALF // GROUP, step, 0)
 
     def modes_copies(k):
@@ -321,24 +364,15 @@
         for row in range(EARLY):
             land[0, layer, low + row] = (early[source, row] * my_scale).astype(BF16)
 
-    for k in range(1, nz):
-        g_copy0(k).wait_recv()
-    g_got0[z] = g_own[pl.ds(pl.multiple_of(z * 16, 16), 16), :]
-    rows = g_got0[0]
-    for i in range(1, nz):
-        rows = rows + g_got0[i]
-    for step_of in (1, 2):
-        count, mine, _ = stages[step_of]
-        g_send[step_of] = rows
-        g_got[step_of, mine] = rows
-        for k in range(1, count):
-            g_copy(step_of, k).start()
-        for k in range(1, count):
-            g_copy(step_of, k).wait_recv()
-        rows = g_got[step_of, 0]
-        for i in range(1, count):
-            rows = rows + g_got[step_of, i]
-    gram_out[...] = rows
+    @pl.when(home)
+    def _():
+        for k in range(1, nz):
+            g_along(k).wait_recv()
+        rows = total(2, nz)
+        g_send[2] = rows
+        gram_out[...] = rows
+        for k in range(1, ny):
+            g_back(k).start()
 
     def deliver(source):
         layer, low = place(source)
@@ -347,32 +381,43 @@
             out[:, c, layer, rows_at, :] = jnp.swapaxes(land[c, layer, rows_at], 0, 1)
 
     deliver(z)
-    for k in order[::-1]:
+    for k in order:
         for copy in modes_copies(k):
             copy.wait_recv()
         deliver(lax.rem(z + nz - k, nz))
+    @pl.when(jnp.logical_not(home))
+    def _():
+        g_back(to_home).wait_recv()
+        g_along(to_home).wait_send()
+
+    @pl.when(home)
+    def _():
+        for k in range(1, ny):
+            g_back(k).wait_send()
+
     for c in (2, 1):
         for side in (0, 1):
             halo(c, side).wait_send()
     for k in order:
-        for c in range(3):
-            part_send(c, k).wait_send()
+        for piece in PIECES:
+            part_send(piece, k).wait_send()
         for copy in modes_copies(k):
             copy.wait_send()
         early_copy(k).wait_send()
-        g_copy0(k).wait_send()
     for step_of, (count, _, _) in enumerate(stages):
         for k in range(1, count):
             e_copy(step_of, k).wait_send()
-            if step_of:
-                g_copy(step_of, k).wait_send()
+    for k in range(1, ny):
+        g_rows(k).wait_send()
+    for k in range(1, nxc):
+        g_across(k).wait_send()
 
 
 def keep(modes, rows, modes_out, rows_out, sem):
-    copies = [
-        pltpu.make_async_copy(modes, modes_out, sem.at[0]),
-        pltpu.make_async_copy(rows, rows_out, sem.at[1]),
-    ]
+    copies = [pltpu.make_async_copy(rows, rows_out, sem.at[8])]
+    for i in range(8):
+        part = pl.ds(2 * i, 2)
+        copies.append(pltpu.make_async_copy(modes.at[part], modes_out.at[part], sem.at[i]))
     for copy in copies:
         copy.start()
     for copy in copies:
@@ -410,12 +455,11 @@
             pltpu.VMEM((3, 8, 128), F32),
             pltpu.VMEM((3, top, 8, 128), F32),
             pltpu.VMEM((128, 128), F32),
-            pltpu.VMEM((nz, 16, 128), F32),
             pltpu.VMEM((3, 16, 128), F32),
             pltpu.VMEM((3, top, 16, 128), F32),
-            dma((6,)), dma((4,)), dma((4,)), dma((3, nz)), dma((3, nz)), dma((2, nz)), dma((2, nz)),
+            dma((6,)), dma((4,)), dma((4,)), dma((4, nz)), dma((4, nz)), dma((2, nz)), dma((2, nz)),
             dma((nz,)), dma((nz,)),
-            dma((3, top)), dma((3, top)), dma((3, top)), dma((3, top)),
+            dma((3, top)), dma((3, top)), dma((4, top)), dma((4, top)),
         ],
         compiler_params=pltpu.CompilerParams(
             collective_id=0, has_side_effects=True, vmem_limit_bytes=48 * 1024 * 1024
@@ -430,7 +474,7 @@
         ),
         in_specs=[any_space, any_space],
         out_specs=(any_space, any_space),
-        scratch_shapes=[dma((2,))],
+        scratch_shapes=[dma((9,))],
         compiler_params=pltpu.CompilerParams(vmem_limit_bytes=1024 * 1024),
         name="keep",
     )(modes, rows)

time: 102 us -> 101 us (level)
  Pallas kernels: 101 us -> 99.7 us
    pallas_call x1, Pallas kernels: 99.8 us -> 98.5 us  [per_device(): pl.pallas_call(functools.partial(kernel, ny, nz, nxc, cells), out_shape=(...]
where the time goes in v3:
time: 101 us; the launch traced here: 100 us
  Pallas kernels  99.7 us (99%)
    pallas_call x1, Pallas kernels, per_device(): pl.pallas_call(functools.partial(kernel, ny, nz, nxc, cells), out_shape=(...  98.5 us

profile of v3, /device:TPU:1, one launch (start us, length us, event | category | flops | bytes accessed | tf_op | source)
XLA Modules:
  0.0 100.4 jit_solution(18205396755967360435)
XLA Ops:
  0.6 98.5 %pod.1 = (bf16[16,3,4,32,128]{4,3,2,1,0:T(8,128)(2,1)S(1)}, f32[16,128]{1,0:T(8,128)S(1)}) custom-call(bf16[16,3,4,32,128]{4,3,2,1,0:T(8,128)(2,1)} %vel.1, f32[3,4,32,128]{3,2,1,0:T(8,128)} %metric_in.1, f32[4,32,128]{2,1,0:T(8,128)} %volume_in.1, bf16[128,128]{1,0:T(8,128)(2,1)} %coeffs_in.1), custom_call_target="tpu_custom_call" | custom-call | tf_op jit(solution)/shard_map/pod/pallas_call | solution.py:432
  99.1 1.2 %keep.1 = (bf16[16,3,4,32,128]{4,3,2,1,0:T(8,128)(2,1)}, f32[16,128]{1,0:T(8,128)}) custom-call(bf16[16,3,4,32,128]{4,3,2,1,0:T(8,128)(2,1)S(1)} %get-tuple-element.6.modes, f32[16,128]{1,0:T(8,128)S(1)} %get-tuple-element.7.rows), custom_call_target="tpu_custom_call" | custom-call | tf_op jit(solution)/shard_map/keep/pallas_call | solution.py:469

commit v4 on v3

--- a/solution.py
+++ b/solution.py
@@ -14,7 +14,8 @@
 HALF = 16
 GROUP = 4
 PIECES = ((0, 0, 16), (1, 0, 16), (2, 0, 12), (2, 12, 4))
-EARLY = 8
+EARLY_PARTS = ((0, 0, 3), (1, 3, 6))
+EARLY = sum(rows for _, _, rows in EARLY_PARTS)
 
 
 def remote(src, dst, send, recv, where):
@@ -49,8 +50,11 @@
         other = lax.rem(q + k, nxc)
         return ((other // 2) * ny + iy) * 2 + lax.rem(other, 2)
 
+    order = [k for pair in zip(range(nz // 2, 0, -1), range(nz // 2 + 1, nz + 1)) for k in pair]
+    order = [k for k in order if k < nz]
+
     barrier = pltpu.get_barrier_semaphore()
-    for k in range(1, nz):
+    for k in order:
         pl.semaphore_signal(barrier, inc=1, device_id={"snap": z_peer(k)}, device_id_type=MESH)
     for k in range(1, ny):
         pl.semaphore_signal(barrier, inc=1, device_id={"space": y_peer(k)}, device_id_type=MESH)
@@ -141,9 +145,6 @@
             a_ss.at[n, k], a_rs.at[n, k], {"snap": peer},
         )
 
-    order = [k for pair in zip(range(nz // 2, 0, -1), range(nz // 2 + 1, nz + 1)) for k in pair]
-    order = [k for k in order if k < nz]
-
     def exchange(piece, ahead=0, enter=None):
         for n, k in enumerate(order):
             part_curl(piece, z_peer(k))
@@ -153,6 +154,8 @@
                     part_send(piece, earlier).start()
             if enter is None or n >= ahead:
                 part_send(piece, k).start()
+            if enter is not None and n == ahead:
+                start_halo()
         part_curl(piece, z, own=True)
 
     def halo(c, side):
@@ -167,6 +170,8 @@
 
     def enter():
         pl.semaphore_wait(barrier, (nz - 1) + (ny - 1) + (nxc - 1) + 2)
+
+    def start_halo():
         for c in (2, 1):
             for side in (0, 1):
                 halo(c, side).start()
@@ -265,11 +270,13 @@
     home = z == iy
     to_home = lax.rem(iy + nz - z, nz)
 
-    def early_copy(k):
+    def early_copy(n, k):
+        _, first, count = EARLY_PARTS[n]
         peer = z_peer(k)
         return remote(
-            raw.at[0, 0:EARLY, pl.ds(pl.multiple_of(peer * 16, 16), 16)], early.at[z],
-            f_ss.at[k], f_rs.at[k], {"snap": peer},
+            raw.at[0, first : first + count, pl.ds(pl.multiple_of(peer * 16, 16), 16)],
+            early.at[z, first : first + count],
+            f_ss.at[n, k], f_rs.at[n, k], {"snap": peer},
         )
 
     for step_of, (count, mine, _) in enumerate(stages):
@@ -277,13 +284,15 @@
         e_got[step_of, mine] = partial_e
         for k in order:
             e_copy(step_of, k).start()
+        for n, (when, _, _) in enumerate(EARLY_PARTS):
+            if when == step_of:
+                for k in order:
+                    early_copy(n, k).start()
         if step_of == 0:
             for k in range(1, ny):
                 g_rows(k).start()
             raw_of(2)
         if step_of == 1:
-            for k in order:
-                early_copy(k).start()
             g_got[0, iy] = g_own[pl.ds(pl.multiple_of(iy * 16, 16), 16), :]
             for k in range(1, ny):
                 g_rows(k).wait_recv()
@@ -358,11 +367,28 @@
 
     my_scale = col[pl.ds(pl.multiple_of(z * 16, 16), 16), :]
     for k in order:
-        early_copy(k).wait_recv()
+        for n in range(len(EARLY_PARTS)):
+            early_copy(n, k).wait_recv()
         source = lax.rem(z + nz - k, nz)
         layer, low = place(source)
         for row in range(EARLY):
             land[0, layer, low + row] = (early[source, row] * my_scale).astype(BF16)
+
+    for c in (2, 1):
+        for side in (0, 1):
+            halo(c, side).wait_send()
+    for k in order:
+        for piece in PIECES:
+            part_send(piece, k).wait_send()
+        for n in range(len(EARLY_PARTS)):
+            early_copy(n, k).wait_send()
+    for step_of, (count, _, _) in enumerate(stages):
+        for k in range(1, count):
+            e_copy(step_of, k).wait_send()
+    for k in range(1, ny):
+        g_rows(k).wait_send()
+    for k in range(1, nxc):
+        g_across(k).wait_send()
 
     @pl.when(home)
     def _():
@@ -385,6 +411,10 @@
         for copy in modes_copies(k):
             copy.wait_recv()
         deliver(lax.rem(z + nz - k, nz))
+    for k in order:
+        for copy in modes_copies(k):
+            copy.wait_send()
+
     @pl.when(jnp.logical_not(home))
     def _():
         g_back(to_home).wait_recv()
@@ -394,23 +424,6 @@
     def _():
         for k in range(1, ny):
             g_back(k).wait_send()
-
-    for c in (2, 1):
-        for side in (0, 1):
-            halo(c, side).wait_send()
-    for k in order:
-        for piece in PIECES:
-            part_send(piece, k).wait_send()
-        for copy in modes_copies(k):
-            copy.wait_send()
-        early_copy(k).wait_send()
-    for step_of, (count, _, _) in enumerate(stages):
-        for k in range(1, count):
-            e_copy(step_of, k).wait_send()
-    for k in range(1, ny):
-        g_rows(k).wait_send()
-    for k in range(1, nxc):
-        g_across(k).wait_send()
 
 
 def keep(modes, rows, modes_out, rows_out, sem):
@@ -458,7 +471,7 @@
             pltpu.VMEM((3, 16, 128), F32),
             pltpu.VMEM((3, top, 16, 128), F32),
             dma((6,)), dma((4,)), dma((4,)), dma((4, nz)), dma((4, nz)), dma((2, nz)), dma((2, nz)),
-            dma((nz,)), dma((nz,)),
+            dma((2, nz)), dma((2, nz)),
             dma((3, top)), dma((3, top)), dma((4, top)), dma((4, top)),
         ],
         compiler_params=pltpu.CompilerParams(

time: 101 us -> 99.2 us (0.982)
  Pallas kernels: 99.7 us -> 98.4 us
    pallas_call x1, Pallas kernels: 98.5 us -> 97.2 us  [per_device(): pl.pallas_call(functools.partial(kernel, ny, nz, nxc, cells), out_shape=(...]
where the time goes in v4:
time: 99.2 us; the launch traced here: 99.1 us
  Pallas kernels  98.4 us (99%)
    pallas_call x1, Pallas kernels, per_device(): pl.pallas_call(functools.partial(kernel, ny, nz, nxc, cells), out_shape=(...  97.2 us

profile of v4, /device:TPU:1, one launch (start us, length us, event | category | flops | bytes accessed | tf_op | source)
XLA Modules:
  0.0 99.1 jit_solution(7076063669865851931)
XLA Ops:
  0.6 97.2 %pod.1 = (bf16[16,3,4,32,128]{4,3,2,1,0:T(8,128)(2,1)S(1)}, f32[16,128]{1,0:T(8,128)S(1)}) custom-call(bf16[16,3,4,32,128]{4,3,2,1,0:T(8,128)(2,1)} %vel.1, f32[3,4,32,128]{3,2,1,0:T(8,128)} %metric_in.1, f32[4,32,128]{2,1,0:T(8,128)} %volume_in.1, bf16[128,128]{1,0:T(8,128)(2,1)} %coeffs_in.1), custom_call_target="tpu_custom_call" | custom-call | tf_op jit(solution)/shard_map/pod/pallas_call | solution.py:445
  97.9 1.2 %keep.1 = (bf16[16,3,4,32,128]{4,3,2,1,0:T(8,128)(2,1)}, f32[16,128]{1,0:T(8,128)}) custom-call(bf16[16,3,4,32,128]{4,3,2,1,0:T(8,128)(2,1)S(1)} %get-tuple-element.6.modes, f32[16,128]{1,0:T(8,128)S(1)} %get-tuple-element.7.rows), custom_call_target="tpu_custom_call" | custom-call | tf_op jit(solution)/shard_map/keep/pallas_call | solution.py:482

commit v5 on v4

--- a/solution.py
+++ b/solution.py
@@ -14,7 +14,7 @@
 HALF = 16
 GROUP = 4
 PIECES = ((0, 0, 16), (1, 0, 16), (2, 0, 12), (2, 12, 4))
-EARLY_PARTS = ((0, 0, 3), (1, 3, 6))
+EARLY_PARTS = ((0, 0, 4), (1, 4, 6))
 EARLY = sum(rows for _, _, rows in EARLY_PARTS)
 
 

time: 99.2 us -> 99 us (level)
  no operation moved by 1% of the time
where the time goes in v5:
time: 99 us; the launch traced here: 98.9 us
  Pallas kernels  98.2 us (99%)
    pallas_call x1, Pallas kernels, per_device(): pl.pallas_call(functools.partial(kernel, ny, nz, nxc, cells), out_shape=(...  97 us

profile of v5, /device:TPU:1, one launch (start us, length us, event | category | flops | bytes accessed | tf_op | source)
XLA Modules:
  0.0 98.9 jit_solution(15304722158254914415)
XLA Ops:
  0.6 97.0 %pod.1 = (bf16[16,3,4,32,128]{4,3,2,1,0:T(8,128)(2,1)S(1)}, f32[16,128]{1,0:T(8,128)S(1)}) custom-call(bf16[16,3,4,32,128]{4,3,2,1,0:T(8,128)(2,1)} %vel.1, f32[3,4,32,128]{3,2,1,0:T(8,128)} %metric_in.1, f32[4,32,128]{2,1,0:T(8,128)} %volume_in.1, bf16[128,128]{1,0:T(8,128)(2,1)} %coeffs_in.1), custom_call_target="tpu_custom_call" | custom-call | tf_op jit(solution)/shard_map/pod/pallas_call | solution.py:445
  97.7 1.2 %keep.1 = (bf16[16,3,4,32,128]{4,3,2,1,0:T(8,128)(2,1)}, f32[16,128]{1,0:T(8,128)}) custom-call(bf16[16,3,4,32,128]{4,3,2,1,0:T(8,128)(2,1)S(1)} %get-tuple-element.6.modes, f32[16,128]{1,0:T(8,128)S(1)} %get-tuple-element.7.rows), custom_call_target="tpu_custom_call" | custom-call | tf_op jit(solution)/shard_map/keep/pallas_call | solution.py:482
